TPU v7x, 512 devices: a whole 4x8x8 slice. The times are simulated.
512 devices in a mesh: cfg: 2 (over core), seq: 64 (over x, z, y_hi), tp: 4 (over y_lo).
Axes of the slice: x: 4, y: 8 (y_hi: 2, y_lo: 4; y = y_hi * 4 + y_lo), z: 8, core: 2. Of those that a mesh axis runs over, the one named last changes fastest.
Arguments:
- stream: bfloat16 [2, 2560, 3072], P('cfg', 'seq', 'tp'), may hold values from -6 to 6
- queries: bfloat16 [2, 2560, 1536], P('cfg', 'seq', 'tp'), may hold values from -6 to 6
- keys: bfloat16 [2, 2560, 1536], P('cfg', 'seq', 'tp'), may hold values from -6 to 6
- values: bfloat16 [2, 2560, 1536], P('cfg', 'seq', 'tp'), may hold values from -6 to 6
- text_keys: bfloat16 [2, 226, 1536], P('cfg', None, 'tp'), may hold values from -6 to 6
- text_values: bfloat16 [2, 226, 1536], P('cfg', None, 'tp'), may hold values from -6 to 6
- out_weight: bfloat16 [1536, 3072], P('tp'), may hold values from -0.15625 to 0.15625
- gate: float32 [3072], P('tp'), may hold values from -4 to 4
- shift: float32 [3072], P('tp'), may hold values from -3 to 3
- scale: float32 [3072], P('tp'), may hold values from -3 to 3
- proj_weight: float32 [3072, 64], P('tp'), may hold values from -0.109375 to 0.109375
- q_gain: float32 [64], replicated, may hold values from 1.4 to 6
- k_gain: float32 [64], replicated, may hold values from 1.4 to 6
- lengths: int32 [64], replicated, may hold values from 1 to 40, 2304 in all
- latents: float32 [2560, 64], P('seq', ('cfg', 'tp')), may hold values from -6 to 6
- alphas: float32 [1000], replicated, may hold values from 0.05 to 0.95
- step_index: int32 [1], replicated, may hold values from 20 to 999
Outputs:
- hidden_out: bfloat16 [2, 2560, 3072], P('cfg', 'seq', 'tp')
- latents_out: float32 [2560, 64], P('seq', ('cfg', 'tp'))
Inputs may be any that keep to these rules, and one draw needn't show every extreme that they name: `lengths`: video tokens held by each index of seq, in token order; they sum to 2304 and the largest is exactly 40. The previous step's entry is step_index - 20.
All inputs are finite; a program needn't handle non-finite values.
Results may differ from a plain program's by a relative error of at most 0.012.
The roundings to bfloat16 on the way count: a program that leaves them out, or rounds other values in their place, can miss the bound.
Values may be sent and summed in bfloat16 or wider, within the bound.
A program may use at most 64 MiB of HBM per device.

v0:
```python
import jax
import jax.numpy as jnp
from jax import lax
from jax.sharding import PartitionSpec as P

D = 3072
HEAD = 64
HP = 30
WP = 45
STRIDE = 20
guide_scale = 6.0
head_eps = 1e-06
final_eps = 1e-05


def partner_2(shard, axis, distance):
    return lax.ppermute(shard, axis, [(i, i ^ 1 << distance) for i in range(lax.axis_size(axis))])


def rope_tables(position):
    frame = position // (HP * WP)
    height = position // WP % HP
    across = position % WP

    def angles(coord, extent):
        freq = 1.0 / 10000.0 ** (jnp.arange(0, extent, 2, dtype=jnp.float32) / extent)
        return coord.astype(jnp.float32)[:, None] * freq[None, :]

    angle = jnp.concatenate([angles(frame, 16), angles(height, 24), angles(across, 24)], axis=1)
    return (jnp.cos(angle), jnp.sin(angle))


def head_norm(field, gain):
    centre = field - jnp.mean(field, axis=-1, keepdims=True)
    spread = jnp.mean(centre * centre, axis=-1, keepdims=True)
    return centre * lax.rsqrt(spread + head_eps) * gain


def rotate_pairs(field, cos_table, sin_table):
    pairs = field.reshape(field.shape[:-1] + (HEAD // 2, 2))
    first = pairs[..., 0]
    second = pairs[..., 1]
    cos_part = cos_table[:, None, :]
    sin_part = sin_table[:, None, :]
    turned = jnp.stack(
        [first * cos_part - second * sin_part, second * cos_part + first * sin_part], axis=-1
    )
    return turned.reshape(field.shape)


def prepare(field, gain, tables):
    count = field.shape[0]
    normed = head_norm(field.astype(jnp.float32).reshape(count, -1, HEAD), gain)
    if tables is not None:
        normed = rotate_pairs(normed, tables[0], tables[1])
    return normed.reshape(count, -1).astype(jnp.bfloat16)


def last_dims(left, right):
    return lax.dot_general(
        left, right, (((1,), (1,)), ((), ())), preferred_element_type=jnp.float32
    )


def shards(
    stream,
    queries,
    keys,
    values,
    text_keys,
    text_values,
    out_weight,
    gate,
    shift,
    scale,
    proj_weight,
    q_gain,
    k_gain,
    lengths,
    latents,
    alphas,
    step_index,
):
    blocks = lax.axis_size("seq")
    group = lax.axis_size("tp")
    rows = queries.shape[1]
    width = queries.shape[2]
    heads_here = width // HEAD
    seq_rank = lax.axis_index("seq")
    order = jnp.arange(blocks, dtype=jnp.int32)
    own_start = jnp.sum(jnp.where(order < seq_rank, lengths, 0))
    own_count = jnp.sum(jnp.where(order == seq_rank, lengths, 0))
    within = jnp.arange(rows, dtype=jnp.int32)
    own_live = within < own_count
    own_tables = rope_tables(own_start + within)
    query_hat = prepare(queries[0], q_gain, own_tables)
    outgoing = keys[0]
    arrived_keys, arrived_values = (
        lax.all_gather(outgoing, "seq", axis=0, tiled=True),
        lax.all_gather(values[0], "seq", axis=0, tiled=True),
    )
    offsets = jnp.cumsum(lengths) - lengths
    all_positions = (offsets[:, None] + within[None, :]).reshape(-1)
    video_keys = prepare(arrived_keys, k_gain, rope_tables(all_positions))
    video_live = (within[None, :] < lengths[:, None]).reshape(-1)
    text_hat = prepare(text_keys[0], k_gain, None)
    text_vals = text_values[0]

    def one_head(head):
        start = head * HEAD
        query_part = lax.dynamic_slice_in_dim(query_hat, start, HEAD, 1)
        video_key_part = lax.dynamic_slice_in_dim(video_keys, start, HEAD, 1)
        video_value_part = lax.dynamic_slice_in_dim(arrived_values, start, HEAD, 1)
        text_key_part = lax.dynamic_slice_in_dim(text_hat, start, HEAD, 1)
        text_value_part = lax.dynamic_slice_in_dim(text_vals, start, HEAD, 1)
        video_scores = last_dims(query_part, video_key_part) * 0.125
        video_scores = jnp.where(video_live[None, :], video_scores, -jnp.inf)
        text_scores = last_dims(query_part, text_key_part) * 0.125
        row_max = jnp.maximum(
            jnp.max(video_scores, axis=1, keepdims=True),
            jnp.max(text_scores, axis=1, keepdims=True),
        )
        video_weights = jnp.exp(video_scores - row_max)
        text_weights = jnp.exp(text_scores - row_max)
        totals = jnp.sum(video_weights, axis=1, keepdims=True) + jnp.sum(
            text_weights, axis=1, keepdims=True
        )
        mixed = jnp.dot(
            video_weights.astype(jnp.bfloat16), video_value_part, preferred_element_type=jnp.float32
        )
        mixed = mixed + jnp.dot(
            text_weights.astype(jnp.bfloat16), text_value_part, preferred_element_type=jnp.float32
        )
        return (mixed / totals).astype(jnp.bfloat16)

    attended = lax.map(one_head, jnp.arange(heads_here, dtype=jnp.int32))
    attended = jnp.transpose(attended, (1, 0, 2)).reshape(rows, width)
    projected = jnp.dot(attended, out_weight, preferred_element_type=jnp.float32)
    summed = lax.psum_scatter(
        projected.astype(jnp.bfloat16), "tp", scatter_dimension=1, tiled=True
    ).astype(jnp.float32)
    hidden = stream[0].astype(jnp.float32) + gate * summed
    hidden = jnp.where(own_live[:, None], hidden, 0.0).astype(jnp.bfloat16)
    widened = lax.optimization_barrier(hidden).astype(jnp.float32)
    row_total, row_square = lax.psum(
        (jnp.sum(widened, axis=1), jnp.sum(widened * widened, axis=1)), "tp"
    )
    mean = row_total[:, None] / D
    square = row_square[:, None] / D
    normed = (widened - mean) * lax.rsqrt(square - mean * mean + final_eps) * (1.0 + scale) + shift
    partial_pred = jnp.dot(
        normed, proj_weight, precision=lax.Precision.HIGHEST, preferred_element_type=jnp.float32
    )
    cfg_rank = lax.axis_index("cfg")
    tp_rank = lax.axis_index("tp")
    piece = proj_weight.shape[1] // (2 * group)
    prediction = lax.psum(partial_pred, "tp")
    partner = partner_2(prediction, "cfg", 0)
    column = (cfg_rank * group + tp_rank) * piece
    mine = lax.dynamic_slice_in_dim(prediction, column, piece, 1)
    theirs = lax.dynamic_slice_in_dim(partner, column, piece, 1)
    is_conditioned = cfg_rank == 0
    conditioned = jnp.where(is_conditioned, mine, theirs)
    unconditioned = jnp.where(is_conditioned, theirs, mine)
    guided = unconditioned + guide_scale * (conditioned - unconditioned)
    current = alphas[step_index[0]]
    earlier = alphas[step_index[0] - STRIDE]
    root_now = jnp.sqrt(current)
    rest_now = jnp.sqrt(1.0 - current)
    clean = root_now * latents - rest_now * guided
    noise = root_now * guided + rest_now * latents
    stepped = jnp.sqrt(earlier) * clean + jnp.sqrt(1.0 - earlier) * noise
    latents_out = jnp.where(own_live[:, None], stepped, 0.0)
    return (hidden[None], latents_out)


def solution(mesh):
    return jax.shard_map(
        shards,
        mesh=mesh,
        in_specs=(
            P("cfg", "seq", "tp"),
            P("cfg", "seq", "tp"),
            P("cfg", "seq", "tp"),
            P("cfg", "seq", "tp"),
            P("cfg", None, "tp"),
            P("cfg", None, "tp"),
            P("tp", None),
            P("tp"),
            P("tp"),
            P("tp"),
            P("tp", None),
            P(),
            P(),
            P(),
            P("seq", ("cfg", "tp")),
            P(),
            P(),
        ),
        out_specs=(P("cfg", "seq", "tp"), P("seq", ("cfg", "tp"))),
        check_vma=False,
    )
```

profile of v0, /device:TPU:1, one launch (start us, length us, event | category | flops | bytes accessed | tf_op | source)
XLA Modules:
  0.0 389.1 jit_solution(11699721490610072539)
XLA Ops:
  9.7 1.3 fusion.51
  18.6 1.4 fusion.29
  20.0 127.2 %all-gather.5.cloned.1.call-done = bf16[1,2560,384]{2,1,0:T(8,128)(2,1)} async-done(((bf16[1,40,384]{2,1,0:T(8,128)(2,1)}), bf16[1,2560,384]{2,1,0:T(8,128)(2,1)}) %all-gather.5.cloned.1.call-update) | async-done | bytes 1966096 | tf_op jit(solution)/shard_map/all_gather | solution.py:99
  147.2 4.0 %copy.54 = bf16[1,2560,384]{1,2,0:T(8,128)(2,1)} copy(bf16[1,2560,384]{2,1,0:T(8,128)(2,1)} %all-gather.5.cloned.1.call-done) | data formatting | bytes 3932160 | tf_op jit(solution)/shard_map/all_gather | solution.py:99
  151.2 3.9 %convert_element_type.154 = f32[1,2560,384]{1,2,0:T(8,128)} convert(bf16[1,2560,384]{1,2,0:T(8,128)(2,1)} %copy.54) | non-fusion elementwise | flops 983040 | bytes 5898240 | tf_op jit(solution)/shard_map/convert_element_type | solution.py:53
  155.1 2.5 reduce_sum.112
  157.6 5.3 %reshape.425 = f32[2560,6,32,2]{0,3,2,1:T(2,128)} reshape(bf16[1,2560,384]{1,2,0:T(8,128)(2,1)} %copy.54) | data formatting | bytes 5898240 | tf_op jit(solution)/shard_map/reshape | solution.py:53
  162.9 2.8 multiply_reduce_fusion
  166.2 1.8 multiply_multiply_fusion
  168.0 5.2 %subtract_convert_fusion = (bf16[2560,6,32,1]{0,3,2,1:T(2,128)(2,1)S(1)}, bf16[2560,6,32,1]{0,3,2,1:T(2,128)(2,1)S(1)}) fusion(f32[2560,6,32,2]{0,3,2,1:T(2,128)S(1)} %multiply_multiply_fusion, f32[2560,32]{0,1:T(8,128)S(1)} %get-tuple-element.135, f32[2560,32]{0,1:T(8,128)S(1)} %get-tuple-element.134), kind=kLoop, calls=%fused_computation.34 | loop fusion | flops 3932160 | bytes 6553600 | tf_op jit(solution)/shard_map/convert.5
  173.2 5.7 %pad_maximum_fusion = bf16[2560,6,32,2]{0,3,2,1:T(2,128)(2,1)} fusion(bf16[2560,6,32,1]{0,3,2,1:T(2,128)(2,1)S(1)} %get-tuple-element.133, bf16[2560,6,32,1]{0,3,2,1:T(2,128)(2,1)S(1)} %get-tuple-element.132), kind=kLoop, calls=%fused_computation.32 | loop fusion | flops 3932160 | bytes 3932160 | tf_op jit(solution)/shard_map/stack | solution.py:45
  178.9 5.2 %convert_element_type.139 = bf16[2560,384]{0,1:T(8,128)(2,1)} reshape(bf16[2560,6,32,2]{0,3,2,1:T(2,128)(2,1)} %pad_maximum_fusion) | data formatting | bytes 3932160 | tf_op jit(solution)/shard_map/convert_element_type | solution.py:56
  184.1 96.8 %all-gather.7.cloned.1.call-done = bf16[1,2560,384]{2,1,0:T(8,128)(2,1)} async-done(((bf16[1,40,384]{2,1,0:T(8,128)(2,1)}), bf16[1,2560,384]{2,1,0:T(8,128)(2,1)}) %all-gather.7.cloned.1.call-update) | async-done | bytes 1966096 | tf_op jit(solution)/shard_map/all_gather | solution.py:100
  281.0 36.7 %while.11 = (s32[]{:T(128)}, bf16[6,40,64]{2,1,0:T(8,128)(2,1)S(1)}, s32[6]{0:T(128)S(1)}, bf16[40,384]{1,0:T(8,128)(2,1)S(1)}, bf16[2560,384]{0,1:T(8,128)(2,1)...) while((s32[]{:T(128)}, ...), condition=%wide.region_14.15_spmd.clone, body=%wide.region_9.14_spmd.clone.sunk | while | flops 29309844 | bytes 2495583 | solution.py:136
  282.4 1.3 fusion.78
  284.5 1.5 fusion.80
  288.5 1.3 fusion.78
  290.6 1.5 fusion.80
  294.6 1.3 fusion.78
  296.8 1.5 fusion.80
  300.8 1.3 fusion.78
  302.9 1.5 fusion.80
  306.9 1.3 fusion.78
  309.0 1.5 fusion.80
  313.0 1.3 fusion.78
  315.1 1.5 fusion.80
  317.9 1.2 convolution_convert_fusion
  319.8 24.9 %reduce-scatter.2.cloned.1.call-done = bf16[40,768]{1,0:T(8,128)(2,1)} async-done(((bf16[40,3072]{1,0:T(8,128)(2,1)}), bf16[40,768]{1,0:T(8,128)(2,1)}) %reduce-scatter.2.cloned.1.call-update) | async-done | bytes 61456 | tf_op jit(solution)/shard_map/reduce_scatter | solution.py:139
  345.8 7.4 %all-reduce = (f32[40]{0:T(128)S(1)}, f32[40]{0:T(128)S(1)}) all-reduce(f32[40]{0:T(128)S(1)} %get-tuple-element.105, f32[40]{0:T(128)S(1)} %get-tuple-element.104), channel_id=1, replica_groups=mesh['cfg'=2,'seq'=64,'tp'=4] {'tp'}, use_global_device_ids=true, to_apply=%region_19.20 | all-reduce | flops 80 | bytes 640 | tf_op jit(solution)/shard_map/psum | solution.py:145
  353.6 13.4 %psum.23 = f32[40,64]{0,1:T(8,128)S(1)} all-reduce(f32[40,64]{0,1:T(8,128)S(1)} %fusion.33), channel_id=1, replica_groups=mesh['cfg'=2,'seq'=64,'tp'=4] {'tp'}, use_global_device_ids=true, to_apply=%region_20.21 | all-reduce | flops 2560 | bytes 20480 | tf_op jit(solution)/shard_map/psum | solution.py:157
  367.0 10.4 %collective-permute-start = (f32[40,64]{0,1:T(8,128)S(1)}, f32[40,64]{0,1:T(8,128)S(1)}, u32[]{:S(2)}, u32[]{:S(2)}) collective-permute-start(f32[40,64]{0,1:T(8,128)S(1)} %psum.23), channel_id=1, source_target_pairs={{0,256},{256,0},{1,257},{257,1},{2,258},{258,2},{3,259},{259,3},{4... | collective-permute-start | bytes 30728 | tf_op jit(solution)/shard_map/ppermute | solution.py:17
  378.0 1.4 fusion.60
  (141 shorter events, 28.9 us)
Async XLA Ops:
  7.2 310.8 %copy-start = (bf16[384,3072]{1,0:T(8,128)(2,1)S(1)}, bf16[384,3072]{1,0:T(8,128)(2,1)}, u32[]{:S(2)}) copy-start(bf16[384,3072]{1,0:T(8,128)(2,1)} %param.25) | copy-start | bytes 7077892
  7.2 11.1 %copy-start.11 = (f32[64]{0:T(128)S(1)}, f32[64]{0:T(128)}, u32[]{:S(2)}) copy-start(f32[64]{0:T(128)} %param.31) | copy-start | bytes 772
  7.2 10.8 %copy-start.4 = (bf16[1,226,384]{2,1,0:T(8,128)(2,1)S(1)}, bf16[1,226,384]{2,1,0:T(8,128)(2,1)}, u32[]{:S(2)}) copy-start(bf16[1,226,384]{2,1,0:T(8,128)(2,1)} %param.23) | copy-start | bytes 520708
  7.2 140.0 %all-gather.5.cloned.1.call-start = ((), (), s32[]{:S(2)}) async-start(), calls=%async_computation.2 | async-start | bytes 1996800 | tf_op jit(solution)/shard_map/all_gather | solution.py:99
  7.9 273.0 %all-gather.7.cloned.1.call-start = ((), (), s32[]{:S(2)}) async-start(), calls=%async_computation.3 | async-start | bytes 1996800 | tf_op jit(solution)/shard_map/all_gather | solution.py:100
  8.7 336.1 %reduce-scatter.2.cloned.1.call-start = ((), (), s32[]{:S(2)}) async-start(), calls=%async_computation.1 | async-start | bytes 307200 | tf_op jit(solution)/shard_map/reduce_scatter | solution.py:139
  162.9 3.3 copy-start.1
  178.9 102.1 %copy-start.6 = (s32[64]{0:T(128)S(1)}, s32[64]{0:T(128)}, u32[]{:S(2)}) copy-start(s32[64]{0:T(128)} %param.32) | copy-start | bytes 772
  317.7 2.1 copy-start.10
  317.7 27.1 %copy-start.5 = (bf16[1,40,768]{2,1,0:T(8,128)(2,1)S(1)}, bf16[1,40,768]{2,1,0:T(8,128)(2,1)}, u32[]{:S(2)}) copy-start(bf16[1,40,768]{2,1,0:T(8,128)(2,1)} %param.19) | copy-start | bytes 184324
  317.7 27.0 %copy-start.8 = (f32[768]{0:T(1024)S(1)}, f32[768]{0:T(1024)}, u32[]{:S(2)}) copy-start(f32[768]{0:T(1024)} %param.26) | copy-start | bytes 9220
  317.7 35.5 %copy-start.3 = (f32[768,64]{0,1:T(8,128)S(1)}, f32[768,64]{0,1:T(8,128)}, u32[]{:S(2)}) copy-start(f32[768,64]{0,1:T(8,128)} %param.29) | copy-start | bytes 589828
  317.7 35.5 %copy-start.7 = (f32[768]{0:T(1024)S(1)}, f32[768]{0:T(1024)}, u32[]{:S(2)}) copy-start(f32[768]{0:T(1024)} %param.27) | copy-start | bytes 9220
  317.8 64.2 %copy-start.9 = (f32[40,8]{0,1:T(8,128)S(1)}, f32[40,8]{0,1:T(8,128)}, u32[]{:S(2)}) copy-start(f32[40,8]{0,1:T(8,128)} %param.33) | copy-start | bytes 3844
  345.7 36.9 %copy-start.2 = (bf16[40,768]{1,0:T(8,128)(2,1)}, bf16[40,768]{1,0:T(8,128)(2,1)S(1)}, u32[]{:S(2)}) copy-start(bf16[40,768]{1,0:T(8,128)(2,1)S(1)} %fusion.37) | copy-start | bytes 184324
  367.0 15.0 %collective-permute-start = (f32[40,64]{0,1:T(8,128)S(1)}, f32[40,64]{0,1:T(8,128)S(1)}, u32[]{:S(2)}, u32[]{:S(2)}) collective-permute-start(f32[40,64]{0,1:T(8,128)S(1)} %psum.23), channel_id=1, source_target_pairs={{0,256},{256,0},{1,257},{257,1},{2,258},{258,2},{3,259},{259,3},{4... | collective-permute-start | bytes 30728 | tf_op jit(solution)/shard_map/ppermute | solution.py:17
Sparse Core Ops, SparseCore 0:
  12.4 134.7 all-gather.4
  151.5 129.3 all-gather.6
  319.3 25.4 reduce-scatter.1
where the time goes:
time: 391 us; the launch traced here: 389 us
  waiting for transfers between devices  250 us (64%)
  other arithmetic  33.5 us (9%)
  matrix products  26.8 us (7%)
  local copies, waits for them, and re-layouts  25.8 us (7%)
  blocking collectives  20.8 us (5%)
  between operations  17.4 us (4%)
  starting transfers between devices  10.5 us (3%)
  loops' own time  4.14 us (1%)
    all_gather x1, waiting for transfers between devices, shards(): lax.all_gather(outgoing, 'seq', axis=0, tiled=True)  127 us
    all_gather x1, waiting for transfers between devices, shards(): lax.all_gather(values[0], 'seq', axis=0, tiled=True)  96.8 us
    reduce_scatter x1, waiting for transfers between devices, shards(): lax.psum_scatter(projected.astype(jnp.bfloat16), 'tp', scatter_dimension=...  24.9 us
    psum x1, blocking collectives, shards(): prediction = lax.psum(partial_pred, 'tp')  13.4 us
    ppermute x1, starting transfers between devices, partner_2(): lax.ppermute(shard, axis, [(i, i ^ 1 << distance) for i in range(lax.axis...  10.4 us
    dot_general x12, matrix products, last_dims(): lax.dot_general(left, right, (((1,), (1,)), ((), ())), preferred_element_...  9.89 us
    dot_general x6, matrix products, one_head(): jnp.dot(video_weights.astype(jnp.bfloat16), video_value_part, preferred_e...  8.91 us
  transfers between devices with their start and end apart: 4, of which 3 were waited for; matrix products, arithmetic and copies ran while one was open for 13% of the time, Pallas kernels for 0%

commit v1 on v0

--- a/solution.py
+++ b/solution.py
@@ -97,7 +97,9 @@
     outgoing = keys[0]
     arrived_keys, arrived_values = (
         lax.all_gather(outgoing, "seq", axis=0, tiled=True),
-        lax.all_gather(values[0], "seq", axis=0, tiled=True),
+        jnp.concatenate(
+            lax.all_to_all(jnp.stack([values[0]] * lax.axis_size("seq")), "seq", 0, 0), axis=0
+        ),
     )
     offsets = jnp.cumsum(lengths) - lengths
     all_positions = (offsets[:, None] + within[None, :]).reshape(-1)

time: 391 us -> 313 us (0.80)
  waiting for transfers between devices: 250 us -> 154 us
  starting transfers between devices: 10.5 us -> 30.4 us
    all_gather x1 -> x0, waiting for transfers between devices: 96.8 us -> none  [shards(): lax.all_gather(values[0], 'seq', axis=0, tiled=True)]
    all_to_all x0 -> x1, starting transfers between devices: none -> 20 us  [shards(): lax.all_to_all(jnp.stack([values[0]] * lax.axis_size('seq')), 'seq', 0, 0)]
  transfers between devices with their start and end apart: 4 -> 4, of which waited for: 3 -> 2; matrix products, arithmetic and copies ran while one was open for 13% -> 15% of each run, Pallas kernels for 0% -> 0%
where the time goes in v1:
time: 313 us; the launch traced here: 312 us
  waiting for transfers between devices  154 us (49%)
  other arithmetic  32.8 us (10%)
  starting transfers between devices  30.4 us (10%)
  matrix products  26.8 us (9%)
  local copies, waits for them, and re-layouts  24.5 us (8%)
  blocking collectives  20.8 us (7%)
  between operations  17.7 us (6%)
  loops' own time  4.14 us (1%)
    all_gather x1, waiting for transfers between devices, shards(): lax.all_gather(outgoing, 'seq', axis=0, tiled=True)  129 us
    reduce_scatter x1, waiting for transfers between devices, shards(): lax.psum_scatter(projected.astype(jnp.bfloat16), 'tp', scatter_dimension=...  24.9 us
    all_to_all x1, starting transfers between devices, shards(): lax.all_to_all(jnp.stack([values[0]] * lax.axis_size('seq')), 'seq', 0, 0)  20 us
    psum x1, blocking collectives, shards(): prediction = lax.psum(partial_pred, 'tp')  13.3 us
    ppermute x1, starting transfers between devices, partner_2(): lax.ppermute(shard, axis, [(i, i ^ 1 << distance) for i in range(lax.axis...  10.4 us
    dot_general x12, matrix products, last_dims(): lax.dot_general(left, right, (((1,), (1,)), ((), ())), preferred_element_...  9.89 us
    dot_general x6, matrix products, one_head(): jnp.dot(video_weights.astype(jnp.bfloat16), video_value_part, preferred_e...  8.91 us
    psum x1, blocking collectives, shards(): lax.psum((jnp.sum(widened, axis=1), jnp.sum(widened * widened, axis=1)),...  7.42 us
  transfers between devices with their start and end apart: 4, of which 2 were waited for; matrix products, arithmetic and copies ran while one was open for 15% of the time, Pallas kernels for 0%

profile of v1, /device:TPU:1, one launch (start us, length us, event | category | flops | bytes accessed | tf_op | source)
XLA Modules:
  0.0 311.6 jit_solution(6255174111129203352)
XLA Ops:
  7.9 2.2 stack.17
  10.1 20.0 %all-to-all-start = ((bf16[64,40,384]{2,1,0:T(8,128)(2,1)}), bf16[64,40,384]{2,1,0:T(8,128)(2,1)}, u32[]{:S(2)}, u32[]{:S(2)}) async-start(bf16[64,40,384]{2,1,0:T(8,128)(2,1)} %stack.17), calls=%async_computation | async-start | bytes 3932160 | tf_op jit(solution)/shard_map/all_to_all | solution.py:101
  35.9 1.4 fusion.29
  37.3 128.8 %all-gather.3.cloned.1.call-done = bf16[1,2560,384]{2,1,0:T(8,128)(2,1)} async-done(((bf16[1,40,384]{2,1,0:T(8,128)(2,1)}), bf16[1,2560,384]{2,1,0:T(8,128)(2,1)}) %all-gather.3.cloned.1.call-update) | async-done | bytes 1966096 | tf_op jit(solution)/shard_map/all_gather | solution.py:99
  166.1 4.0 %copy.54 = bf16[1,2560,384]{1,2,0:T(8,128)(2,1)} copy(bf16[1,2560,384]{2,1,0:T(8,128)(2,1)} %all-gather.3.cloned.1.call-done) | data formatting | bytes 3932160 | tf_op jit(solution)/shard_map/all_gather | solution.py:99
  170.1 3.9 %convert_element_type.154 = f32[1,2560,384]{1,2,0:T(8,128)} convert(bf16[1,2560,384]{1,2,0:T(8,128)(2,1)} %copy.54) | non-fusion elementwise | flops 983040 | bytes 5898240 | tf_op jit(solution)/shard_map/convert_element_type | solution.py:53
  174.1 2.5 reduce_sum.112
  176.6 5.3 %reshape.429 = f32[2560,6,32,2]{0,3,2,1:T(2,128)} reshape(bf16[1,2560,384]{1,2,0:T(8,128)(2,1)} %copy.54) | data formatting | bytes 5898240 | tf_op jit(solution)/shard_map/reshape | solution.py:53
  181.9 2.8 multiply_reduce_fusion
  185.2 1.8 multiply_multiply_fusion
  187.0 5.2 %subtract_convert_fusion = (bf16[2560,6,32,1]{0,3,2,1:T(2,128)(2,1)S(1)}, bf16[2560,6,32,1]{0,3,2,1:T(2,128)(2,1)S(1)}) fusion(f32[2560,6,32,2]{0,3,2,1:T(2,128)S(1)} %multiply_multiply_fusion, f32[2560,32]{0,1:T(8,128)S(1)} %get-tuple-element.135, f32[2560,32]{0,1:T(8,128)S(1)} %get-tuple-element.134), kind=kLoop, calls=%fused_computation.34 | loop fusion | flops 3932160 | bytes 6553600 | tf_op jit(solution)/shard_map/convert.5
  192.1 5.7 %pad_maximum_fusion = bf16[2560,6,32,2]{0,3,2,1:T(2,128)(2,1)} fusion(bf16[2560,6,32,1]{0,3,2,1:T(2,128)(2,1)S(1)} %get-tuple-element.133, bf16[2560,6,32,1]{0,3,2,1:T(2,128)(2,1)S(1)} %get-tuple-element.132), kind=kLoop, calls=%fused_computation.32 | loop fusion | flops 3932160 | bytes 3932160 | tf_op jit(solution)/shard_map/stack | solution.py:45
  197.9 5.2 %convert_element_type.139 = bf16[2560,384]{0,1:T(8,128)(2,1)} reshape(bf16[2560,6,32,2]{0,3,2,1:T(2,128)(2,1)} %pad_maximum_fusion) | data formatting | bytes 3932160 | tf_op jit(solution)/shard_map/convert_element_type | solution.py:56
  203.1 36.7 %while.11 = (s32[]{:T(128)}, bf16[6,40,64]{2,1,0:T(8,128)(2,1)S(1)}, s32[6]{0:T(128)S(1)}, bf16[40,384]{1,0:T(8,128)(2,1)S(1)}, bf16[2560,384]{0,1:T(8,128)(2,1)...) while((s32[]{:T(128)}, ...), condition=%wide.region_14.15_spmd.clone, body=%wide.region_9.14_spmd.clone.sunk | while | flops 29309844 | bytes 2495583 | solution.py:138
  204.5 1.3 fusion.78
  206.6 1.5 fusion.80
  210.6 1.3 fusion.78
  212.8 1.5 fusion.80
  216.8 1.3 fusion.78
  218.9 1.5 fusion.80
  222.9 1.3 fusion.78
  225.0 1.5 fusion.80
  229.0 1.3 fusion.78
  231.1 1.5 fusion.80
  235.2 1.3 fusion.78
  237.3 1.5 fusion.80
  240.1 1.2 convolution_convert_fusion
  242.0 24.9 %reduce-scatter.2.cloned.1.call-done = bf16[40,768]{1,0:T(8,128)(2,1)} async-done(((bf16[40,3072]{1,0:T(8,128)(2,1)}), bf16[40,768]{1,0:T(8,128)(2,1)}) %reduce-scatter.2.cloned.1.call-update) | async-done | bytes 61456 | tf_op jit(solution)/shard_map/reduce_scatter | solution.py:141
  267.9 7.4 %all-reduce = (f32[40]{0:T(128)S(1)}, f32[40]{0:T(128)S(1)}) all-reduce(f32[40]{0:T(128)S(1)} %get-tuple-element.105, f32[40]{0:T(128)S(1)} %get-tuple-element.104), channel_id=1, replica_groups=mesh['cfg'=2,'seq'=64,'tp'=4] {'tp'}, use_global_device_ids=true, to_apply=%region_19.20 | all-reduce | flops 80 | bytes 640 | tf_op jit(solution)/shard_map/psum | solution.py:147
  275.8 13.3 %psum.23 = f32[40,64]{0,1:T(8,128)S(1)} all-reduce(f32[40,64]{0,1:T(8,128)S(1)} %fusion.33), channel_id=1, replica_groups=mesh['cfg'=2,'seq'=64,'tp'=4] {'tp'}, use_global_device_ids=true, to_apply=%region_20.21 | all-reduce | flops 2560 | bytes 20480 | tf_op jit(solution)/shard_map/psum | solution.py:159
  289.1 10.4 %collective-permute-start = (f32[40,64]{0,1:T(8,128)S(1)}, f32[40,64]{0,1:T(8,128)S(1)}, u32[]{:S(2)}, u32[]{:S(2)}) collective-permute-start(f32[40,64]{0,1:T(8,128)S(1)} %psum.23), channel_id=1, source_target_pairs={{0,256},{256,0},{1,257},{257,1},{2,258},{258,2},{3,259},{259,3},{4... | collective-permute-start | bytes 30728 | tf_op jit(solution)/shard_map/ppermute | solution.py:17
  300.2 1.4 fusion.60
  (145 shorter events, 25.3 us)
Async XLA Ops:
  7.2 232.9 %copy-start = (bf16[384,3072]{1,0:T(8,128)(2,1)S(1)}, bf16[384,3072]{1,0:T(8,128)(2,1)}, u32[]{:S(2)}) copy-start(bf16[384,3072]{1,0:T(8,128)(2,1)} %param.25) | copy-start | bytes 7077892
  7.2 158.9 %all-gather.3.cloned.1.call-start = ((), (), s32[]{:S(2)}) async-start(), calls=%async_computation.3 | async-start | bytes 1996800 | tf_op jit(solution)/shard_map/all_gather | solution.py:99
  10.1 20.0 %copy-start.7 = (s32[64]{0:T(128)S(1)}, s32[64]{0:T(128)}, u32[]{:S(2)}) copy-start(s32[64]{0:T(128)} %param.32) | copy-start | bytes 772
  10.1 22.6 %copy-start.5 = (bf16[1,40,384]{2,1,0:T(8,128)(2,1)S(1)}, bf16[1,40,384]{2,1,0:T(8,128)(2,1)}, u32[]{:S(2)}) copy-start(bf16[1,40,384]{2,1,0:T(8,128)(2,1)} %param.20) | copy-start | bytes 92164
  10.1 23.3 %copy-start.12 = (f32[64]{0:T(128)S(1)}, f32[64]{0:T(128)}, u32[]{:S(2)}) copy-start(f32[64]{0:T(128)} %param.31) | copy-start | bytes 772
  10.1 24.0 %copy-start.13 = (f32[64]{0:T(128)S(1)}, f32[64]{0:T(128)}, u32[]{:S(2)}) copy-start(f32[64]{0:T(128)} %param.30) | copy-start | bytes 772
  10.1 193.0 %all-to-all-start = ((bf16[64,40,384]{2,1,0:T(8,128)(2,1)}), bf16[64,40,384]{2,1,0:T(8,128)(2,1)}, u32[]{:S(2)}, u32[]{:S(2)}) async-start(bf16[64,40,384]{2,1,0:T(8,128)(2,1)} %stack.17), calls=%async_computation | async-start | bytes 3932160 | tf_op jit(solution)/shard_map/all_to_all | solution.py:101
  30.1 5.1 %copy-start.4 = (bf16[1,226,384]{2,1,0:T(8,128)(2,1)S(1)}, bf16[1,226,384]{2,1,0:T(8,128)(2,1)}, u32[]{:S(2)}) copy-start(bf16[1,226,384]{2,1,0:T(8,128)(2,1)} %param.23) | copy-start | bytes 520708
  30.1 236.8 %reduce-scatter.2.cloned.1.call-start = ((), (), s32[]{:S(2)}) async-start(), calls=%async_computation.2 | async-start | bytes 307200 | tf_op jit(solution)/shard_map/reduce_scatter | solution.py:141
  181.9 3.3 %copy-start.1 = (f32[2560,6,32,2]{0,3,2,1:T(2,128)S(1)}, f32[2560,6,32,2]{0,3,2,1:T(2,128)}, u32[]{:S(2)}) copy-start(f32[2560,6,32,2]{0,3,2,1:T(2,128)} %reshape.429) | copy-start | bytes 11796484
  239.8 2.1 copy-start.11
  239.8 27.1 %copy-start.6 = (bf16[1,40,768]{2,1,0:T(8,128)(2,1)S(1)}, bf16[1,40,768]{2,1,0:T(8,128)(2,1)}, u32[]{:S(2)}) copy-start(bf16[1,40,768]{2,1,0:T(8,128)(2,1)} %param.19) | copy-start | bytes 184324
  239.9 27.0 %copy-start.9 = (f32[768]{0:T(1024)S(1)}, f32[768]{0:T(1024)}, u32[]{:S(2)}) copy-start(f32[768]{0:T(1024)} %param.26) | copy-start | bytes 9220
  239.9 35.5 %copy-start.3 = (f32[768,64]{0,1:T(8,128)S(1)}, f32[768,64]{0,1:T(8,128)}, u32[]{:S(2)}) copy-start(f32[768,64]{0,1:T(8,128)} %param.29) | copy-start | bytes 589828
  239.9 35.5 %copy-start.8 = (f32[768]{0:T(1024)S(1)}, f32[768]{0:T(1024)}, u32[]{:S(2)}) copy-start(f32[768]{0:T(1024)} %param.27) | copy-start | bytes 9220
  239.9 64.2 %copy-start.10 = (f32[40,8]{0,1:T(8,128)S(1)}, f32[40,8]{0,1:T(8,128)}, u32[]{:S(2)}) copy-start(f32[40,8]{0,1:T(8,128)} %param.33) | copy-start | bytes 3844
  267.8 36.9 %copy-start.2 = (bf16[40,768]{1,0:T(8,128)(2,1)}, bf16[40,768]{1,0:T(8,128)(2,1)S(1)}, u32[]{:S(2)}) copy-start(bf16[40,768]{1,0:T(8,128)(2,1)S(1)} %fusion.37) | copy-start | bytes 184324
  289.1 15.0 %collective-permute-start = (f32[40,64]{0,1:T(8,128)S(1)}, f32[40,64]{0,1:T(8,128)S(1)}, u32[]{:S(2)}, u32[]{:S(2)}) collective-permute-start(f32[40,64]{0,1:T(8,128)S(1)} %psum.23), channel_id=1, source_target_pairs={{0,256},{256,0},{1,257},{257,1},{2,258},{258,2},{3,259},{259,3},{4... | collective-permute-start | bytes 30728 | tf_op jit(solution)/shard_map/ppermute | solution.py:17
Sparse Core Ops, SparseCore 0:
  12.3 153.7 all-gather.2
  241.4 25.4 reduce-scatter.1
